TPU v7x, 512 devices: a whole 4x4x16 slice. The times are simulated.
512 devices in a mesh: dp: 128 (over z, x, core), mp: 4 (over y).
Axes of the slice: x: 4, y: 4, z: 16, core: 2. Of those that a mesh axis runs over, the one named last changes fastest.
Arguments:
- session_length: int32 [128], P('dp'), may hold values from 1 to 128
- event_owner: int32 [16384, 1], P('dp'), may hold values from 0 to 127; in each aligned block of 128 rows (0 to 127, 128 to 255, ...) at most 2 rows name the same one
- event_row: int32 [16384], P('dp'), may hold values from 0 to 255
- text_rows: bfloat16 [32768, 4096], P('dp', 'mp'), may hold values from -6 to 6
- image_rows: bfloat16 [32768, 4096], P('dp', 'mp'), may hold values from -6 to 6
- price: float32 [32768], P('dp'), may hold values from 0.2 to 5
- price_dir: bfloat16 [4096], P('mp'), may hold values from -4 to 4
- norm_gain: bfloat16 [4096], P('mp'), may hold values from 0.5 to 1.5
- w_query: bfloat16 [4096, 2048], P('dp', 'mp'), may hold values from -1 to 1
- w_key: bfloat16 [4096, 2048], P('dp', 'mp'), may hold values from -1 to 1
- w_value: bfloat16 [4096, 2048], P('dp', 'mp'), may hold values from -0.09375 to 0.09375
- cotangent: bfloat16 [16384, 4096], P('dp', 'mp'), may hold values from -6 to 6
Outputs:
- context: bfloat16 [16384, 2048], P('dp', 'mp')
- text_grad: float32 [32768, 4096], P('dp', 'mp')
- image_grad: float32 [32768, 4096], P('dp', 'mp')
Inputs may be any that keep to these rules, and one draw needn't show every extreme that they name: `event_owner`: among the event slots of one index of dp, no owner is named more than 2 times, a bound that some block reaches.
All inputs are finite; a program needn't handle non-finite values.
Results may differ from a plain program's by a relative error of at most 0.0063.
Values may be sent and summed in bfloat16 or wider, within the bound.
No kernel may reach another device: no remote copies, remote signals or barrier semaphores. Data moves between devices by JAX's collectives and lax.ppermute only.
A program may use at most 64 MiB of HBM per device.

v0:
```python
import math
import jax
import jax.numpy as jnp
from jax import lax
from jax.sharding import PartitionSpec as P

HD = 128
SLOT = 128


def one_hot(rows, columns):
    return (rows[:, None] == columns[None, :]).astype(jnp.bfloat16)


def pick(selector, values):
    return jnp.dot(selector, values, preferred_element_type=jnp.float32)


def attend(query, keys, values, session_length):
    heads_here = query.shape[1] // HD
    shape3 = (SLOT, heads_here, HD)
    scores = jnp.einsum(
        "qhd,khd->hqk",
        query.reshape(shape3),
        keys.reshape(shape3),
        preferred_element_type=jnp.float32,
    ) / math.sqrt(HD)
    position = jnp.arange(SLOT, dtype=jnp.int32)
    live_mask = position < session_length[0]
    allowed = (position[None, :] <= position[:, None])[None] & live_mask[None, None, :]
    scores = jnp.where(allowed, scores, jnp.float32(-1e30))
    row_max = jnp.max(scores, axis=-1, keepdims=True)
    powers = jnp.exp(scores - row_max)
    probs = (powers / jnp.sum(powers, axis=-1, keepdims=True)).astype(jnp.bfloat16)
    context = jnp.einsum(
        "hqk,khd->qhd", probs, values.reshape(shape3), preferred_element_type=jnp.float32
    )
    context = jnp.where(live_mask[:, None, None], context, jnp.float32(0.0))
    return context.reshape(SLOT, heads_here * HD).astype(jnp.bfloat16)


def local(
    session_length,
    event_owner,
    event_row,
    text_rows,
    image_rows,
    price,
    price_dir,
    norm_gain,
    w_query,
    w_key,
    w_value,
    cotangent,
):
    peers = lax.axis_size("dp")
    parts = lax.axis_size("mp")
    mine = lax.axis_index("mp")
    tok_count = event_row.shape[0]
    capacity = 2 * tok_count // peers
    col_width = text_rows.shape[1]
    table_rows = text_rows.shape[0]
    slots = jnp.arange(peers * capacity, dtype=jnp.int32)
    weights = lax.all_gather(
        jnp.concatenate([w_query, w_key, w_value], axis=1), "dp", axis=0, tiled=True
    )
    owner_ids = event_owner[:, 0]
    place = jnp.arange(tok_count, dtype=jnp.int32)
    same = (owner_ids[:, None] == owner_ids[None, :]) & (place[None, :] < place[:, None])
    slot_ids = owner_ids * capacity + jnp.sum(same.astype(jnp.int32), axis=1)
    taken = slots[:, None] == slot_ids[None, :]
    requests = (jnp.sum(jnp.where(taken, event_row[None, :] + 1, 0), axis=1) - 1).reshape(
        peers, capacity
    )
    got_ids = lax.all_to_all(requests, "dp", split_axis=0, concat_axis=0, tiled=True).reshape(-1)
    text_float = text_rows.astype(jnp.float32)
    image_float = image_rows.astype(jnp.float32)
    table = (
        text_float * image_float + price[:, None] * price_dir.astype(jnp.float32)[None, :]
    ).astype(jnp.bfloat16)
    wanted = one_hot(got_ids, jnp.arange(table_rows, dtype=jnp.int32))
    replies = lax.all_to_all(
        pick(wanted, table).astype(jnp.bfloat16).reshape(peers, capacity, col_width),
        "dp",
        split_axis=0,
        concat_axis=0,
        tiled=True,
    ).reshape(peers * capacity, col_width)
    grad_buffer = pick(taken.astype(jnp.bfloat16), cotangent).astype(jnp.bfloat16)
    grad_buffer, replies = lax.optimization_barrier((grad_buffer, replies))
    got_grads = lax.all_to_all(
        grad_buffer.reshape(peers, capacity, col_width),
        "dp",
        split_axis=0,
        concat_axis=0,
        tiled=True,
    ).reshape(peers * capacity, col_width)
    row_sums = pick(wanted.T, got_grads)
    text_grad = row_sums * image_float
    image_grad = row_sums * text_float
    joined = pick(one_hot(slot_ids, slots), replies).astype(jnp.bfloat16)
    turns = [
        (
            joined
            if k == 0
            else lax.ppermute(joined, "mp", [(i, (i + k) % parts) for i in range(parts)])
        )
        for k in range(parts)
    ]
    stacked = jnp.stack(turns)
    features = jnp.concatenate(
        [
            lax.dynamic_index_in_dim(stacked, (mine - s) % parts, 0, keepdims=False)
            for s in range(parts)
        ],
        axis=1,
    ).astype(jnp.float32)
    gain = lax.all_gather(norm_gain, "mp", axis=0, tiled=True).astype(jnp.float32)
    scale = lax.rsqrt(jnp.mean(features * features, axis=1, keepdims=True) + 1e-06)
    normed = (features * scale * gain[None, :]).astype(jnp.bfloat16)
    projected = jnp.dot(normed, weights, preferred_element_type=jnp.float32).astype(jnp.bfloat16)
    width = w_query.shape[1]
    context = attend(
        projected[:, :width],
        projected[:, width : 2 * width],
        projected[:, 2 * width :],
        session_length,
    )
    return (context, text_grad, image_grad)


def solution(mesh):
    return jax.shard_map(
        local,
        mesh=mesh,
        in_specs=(
            P("dp"),
            P("dp", None),
            P("dp"),
            P("dp", "mp"),
            P("dp", "mp"),
            P("dp"),
            P("mp"),
            P("mp"),
            P("dp", "mp"),
            P("dp", "mp"),
            P("dp", "mp"),
            P("dp", "mp"),
        ),
        out_specs=(P("dp", "mp"), P("dp", "mp"), P("dp", "mp")),
        check_vma=False,
    )
```

profile of v0, /device:TPU:1, one launch (start us, length us, event | category | flops | bytes accessed | tf_op | source)
XLA Modules:
  0.0 196.3 jit_solution(1731019495664114980)
XLA Ops:
  7.2 1.5 pad_maximum_fusion.3
  8.7 0.9 convert_reduce_fusion
  9.6 0.7 multiply_add_fusion
  10.4 0.8 sub.24
  11.2 20.4 %all-to-all-start = ((s32[128,1,2]{2,1,0:T(1,128)}), s32[128,1,2]{2,1,0:T(1,128)S(1)}, u32[]{:S(2)}, u32[]{:S(2)}) async-start(s32[128,1,2]{2,1,0:T(1,128)} %bitcast.4), calls=%async_computation | async-start | bytes 131072 | tf_op jit(solution)/shard_map/all_to_all | solution.py:75
  31.6 0.7 convert_element_type.55
  32.3 14.1 %all-to-all-done = s32[128,1,2]{2,1,0:T(1,128)S(1)} async-done(((s32[128,1,2]{2,1,0:T(1,128)}), s32[128,1,2]{2,1,0:T(1,128)S(1)}, u32[]{:S(2)}, u32[]{:S(2)}) %all-to-all-start) | async-done | bytes 1056 | tf_op jit(solution)/shard_map/all_to_all | solution.py:75
  46.4 0.5 broadcast.75
  47.0 0.8 reduce.3
  47.9 1.7 convolution_convert_fusion.1
  49.6 1.0 reshape.110
  50.6 5.7 %all-to-all-start.1 = ((bf16[128,2,1024]{2,1,0:T(2,128)(2,1)}), bf16[128,2,1024]{2,1,0:T(2,128)(2,1)S(1)}, u32[]{:S(2)}, u32[]{:S(2)}) async-start(bf16[128,2,1024]{2,1,0:T(2,128)(2,1)} %reshape.110), calls=%async_computation.1 | async-start | bytes 1048576 | tf_op jit(solution)/shard_map/all_to_all | solution.py:82
  56.6 33.6 %all-to-all-done.1 = bf16[128,2,1024]{2,1,0:T(2,128)(2,1)S(1)} async-done(((bf16[128,2,1024]{2,1,0:T(2,128)(2,1)}), bf16[128,2,1024]{2,1,0:T(2,128)(2,1)S(1)}, u32[]{:S(2)}, u32[]{:S(2)}) %all-to-all-start.1) | async-done | bytes 524320 | tf_op jit(solution)/shard_map/all_to_all | solution.py:82
  90.4 1.0 reshape.115
  91.3 9.5 %all-to-all-start.2 = ((bf16[128,2,1024]{2,1,0:T(2,128)(2,1)}), bf16[128,2,1024]{2,1,0:T(2,128)(2,1)S(1)}, u32[]{:S(2)}, u32[]{:S(2)}) async-start(bf16[128,2,1024]{2,1,0:T(2,128)(2,1)} %reshape.115), calls=%async_computation.2 | async-start | bytes 1048576 | tf_op jit(solution)/shard_map/all_to_all | solution.py:91
  101.8 3.2 %collective-permute-start = (bf16[128,1024]{1,0:T(8,128)(2,1)S(1)}, bf16[128,1024]{1,0:T(8,128)(2,1)S(1)}, u32[]{:S(2)}, u32[]{:S(2)}) collective-permute-start(bf16[128,1024]{1,0:T(8,128)(2,1)S(1)} %convolution_convert_fusion.3), channel_id=1, source_target_pairs={{0,1},{1,2},{2,3},{3,0},{4,5},{5,6},{6,7},{7,4},{8,9},{9,10},{10,1... | collective-permute-start | bytes 786440 | tf_op jit(solution)/shard_map/ppermute | solution.py:106
  105.0 4.4 %collective-permute-start.1 = (bf16[128,1024]{1,0:T(8,128)(2,1)S(1)}, bf16[128,1024]{1,0:T(8,128)(2,1)S(1)}, u32[]{:S(2)}, u32[]{:S(2)}) collective-permute-start(bf16[128,1024]{1,0:T(8,128)(2,1)S(1)} %convolution_convert_fusion.3), channel_id=1, source_target_pairs={{0,2},{1,3},{2,0},{3,1},{4,6},{5,7},{6,4},{7,5},{8,10},{9,11},{10,... | collective-permute-start | bytes 786440 | tf_op jit(solution)/shard_map/ppermute | solution.py:106
  109.4 3.0 %collective-permute-start.2 = (bf16[128,1024]{1,0:T(8,128)(2,1)S(1)}, bf16[128,1024]{1,0:T(8,128)(2,1)S(1)}, u32[]{:S(2)}, u32[]{:S(2)}) collective-permute-start(bf16[128,1024]{1,0:T(8,128)(2,1)S(1)} %convolution_convert_fusion.3), channel_id=1, source_target_pairs={{0,3},{1,0},{2,1},{3,2},{4,7},{5,4},{6,5},{7,6},{8,11},{9,8},{10,9... | collective-permute-start | bytes 786440 | tf_op jit(solution)/shard_map/ppermute | solution.py:106
  112.5 13.0 %all_gather.6 = bf16[4096]{0:T(1024)(128)(2,1)S(1)} all-gather(bf16[1024]{0:T(1024)(128)(2,1)S(1)} %copy-done.3), channel_id=1, replica_groups=mesh['dp'=128,'mp'=4] {'mp'}, dimensions={0}, use_global_device_ids=true | all-gather | bytes 10240 | tf_op jit(solution)/shard_map/all_gather | solution.py:118
  126.3 7.7 %all-to-all-done.2 = bf16[128,2,1024]{2,1,0:T(2,128)(2,1)S(1)} async-done(((bf16[128,2,1024]{2,1,0:T(2,128)(2,1)}), bf16[128,2,1024]{2,1,0:T(2,128)(2,1)S(1)}, u32[]{:S(2)}, u32[]{:S(2)}) %all-to-all-start.2) | async-done | bytes 524320 | tf_op jit(solution)/shard_map/all_to_all | solution.py:91
  134.3 1.7 convert_multiply_fusion.4
  136.0 45.6 %all-gather.2.cloned.1.call-done = bf16[4096,1536]{1,0:T(8,128)(2,1)} async-done(((bf16[32,1536]{1,0:T(8,128)(2,1)}), bf16[4096,1536]{1,0:T(8,128)(2,1)}) %all-gather.2.cloned.1.call-update) | async-done | bytes 12582928 | tf_op jit(solution)/shard_map/all_gather | solution.py:64
  181.6 6.4 %convolution_convert_fusion = bf16[128,1536]{1,0:T(8,128)(2,1)S(1)} fusion(bf16[4096,1536]{1,0:T(8,128)(2,1)} %all-gather.2.cloned.1.call-done, f32[4096]{0:T(1024)S(1)} %convert_element_type.60, f32[128]{0:T(128)S(1)} %add_rsqrt_fusion, bf16[128,1024]{1,0:T(8,128)(2,1)S(1)} %get-tuple-element.22, bf16[128,1024]{1,0:T(8,128)(2,1)S(1)} %get-tuple-element.23, ...), kind=kOutput, calls=%fused_computation.3 | convolution fusion | flops 1616576512 | bytes 14041600 | tf_op jit(solution)/shard_map/dot_general | solution.py:121
  188.7 0.8 copy.36
  (35 shorter events, 2.6 us)
Async XLA Ops:
  7.2 49.1 %copy-start = (bf16[128,1024]{1,0:T(8,128)(2,1)S(1)}, bf16[128,1024]{1,0:T(8,128)(2,1)}, u32[]{:S(2)}) copy-start(bf16[128,1024]{1,0:T(8,128)(2,1)} %param.23) | copy-start | bytes 786436
  7.2 174.4 %all-gather.2.cloned.1.call-start = ((), (), s32[]{:S(2)}) async-start(), calls=%async_computation.3 | async-start | bytes 12681216 | tf_op jit(solution)/shard_map/all_gather | solution.py:64
  11.2 35.2 %all-to-all-start = ((s32[128,1,2]{2,1,0:T(1,128)}), s32[128,1,2]{2,1,0:T(1,128)S(1)}, u32[]{:S(2)}, u32[]{:S(2)}) async-start(s32[128,1,2]{2,1,0:T(1,128)} %bitcast.4), calls=%async_computation | async-start | bytes 131072 | tf_op jit(solution)/shard_map/all_to_all | solution.py:75
  50.6 39.6 %all-to-all-start.1 = ((bf16[128,2,1024]{2,1,0:T(2,128)(2,1)}), bf16[128,2,1024]{2,1,0:T(2,128)(2,1)S(1)}, u32[]{:S(2)}, u32[]{:S(2)}) async-start(bf16[128,2,1024]{2,1,0:T(2,128)(2,1)} %reshape.110), calls=%async_computation.1 | async-start | bytes 1048576 | tf_op jit(solution)/shard_map/all_to_all | solution.py:82
  56.3 45.3 %copy-start.4 = (s32[128,1]{0,1:T(1,128)S(1)}, s32[128,1]{0,1:T(1,128)}, u32[]{:S(2)}) copy-start(s32[128,1]{0,1:T(1,128)} %param.13) | copy-start | bytes 1540
  56.6 56.0 %copy-start.3 = (bf16[1024]{0:T(1024)(128)(2,1)S(1)}, bf16[1024]{0:T(1024)(128)(2,1)}, u32[]{:S(2)}) copy-start(bf16[1024]{0:T(1024)(128)(2,1)} %param.19) | copy-start | bytes 6148
  91.3 42.7 %all-to-all-start.2 = ((bf16[128,2,1024]{2,1,0:T(2,128)(2,1)}), bf16[128,2,1024]{2,1,0:T(2,128)(2,1)S(1)}, u32[]{:S(2)}, u32[]{:S(2)}) async-start(bf16[128,2,1024]{2,1,0:T(2,128)(2,1)} %reshape.115), calls=%async_computation.2 | async-start | bytes 1048576 | tf_op jit(solution)/shard_map/all_to_all | solution.py:91
  101.8 23.9 %collective-permute-start = (bf16[128,1024]{1,0:T(8,128)(2,1)S(1)}, bf16[128,1024]{1,0:T(8,128)(2,1)S(1)}, u32[]{:S(2)}, u32[]{:S(2)}) collective-permute-start(bf16[128,1024]{1,0:T(8,128)(2,1)S(1)} %convolution_convert_fusion.3), channel_id=1, source_target_pairs={{0,1},{1,2},{2,3},{3,0},{4,5},{5,6},{6,7},{7,4},{8,9},{9,10},{10,1... | collective-permute-start | bytes 786440 | tf_op jit(solution)/shard_map/ppermute | solution.py:106
  105.0 20.7 %collective-permute-start.1 = (bf16[128,1024]{1,0:T(8,128)(2,1)S(1)}, bf16[128,1024]{1,0:T(8,128)(2,1)S(1)}, u32[]{:S(2)}, u32[]{:S(2)}) collective-permute-start(bf16[128,1024]{1,0:T(8,128)(2,1)S(1)} %convolution_convert_fusion.3), channel_id=1, source_target_pairs={{0,2},{1,3},{2,0},{3,1},{4,6},{5,7},{6,4},{7,5},{8,10},{9,11},{10,... | collective-permute-start | bytes 786440 | tf_op jit(solution)/shard_map/ppermute | solution.py:106
  109.4 16.3 %collective-permute-start.2 = (bf16[128,1024]{1,0:T(8,128)(2,1)S(1)}, bf16[128,1024]{1,0:T(8,128)(2,1)S(1)}, u32[]{:S(2)}, u32[]{:S(2)}) collective-permute-start(bf16[128,1024]{1,0:T(8,128)(2,1)S(1)} %convolution_convert_fusion.3), channel_id=1, source_target_pairs={{0,3},{1,0},{2,1},{3,2},{4,7},{5,4},{6,5},{7,6},{8,11},{9,8},{10,9... | collective-permute-start | bytes 786440 | tf_op jit(solution)/shard_map/ppermute | solution.py:106
  125.9 8.4 %copy-start.1 = (bf16[256,1024]{1,0:T(8,128)(2,1)S(1)}, bf16[256,1024]{1,0:T(8,128)(2,1)}, u32[]{:S(2)}) copy-start(bf16[256,1024]{1,0:T(8,128)(2,1)} %param.16) | copy-start | bytes 1572868
  125.9 8.4 %copy-start.2 = (bf16[256,1024]{1,0:T(8,128)(2,1)S(1)}, bf16[256,1024]{1,0:T(8,128)(2,1)}, u32[]{:S(2)}) copy-start(bf16[256,1024]{1,0:T(8,128)(2,1)} %param.15) | copy-start | bytes 1572868
Sparse Core Ops, SparseCore 0:
  11.7 169.7 all-gather.1
where the time goes:
time: 197 us; the launch traced here: 196 us
  waiting for transfers between devices  101 us (51%)
  starting transfers between devices  46.2 us (23%)
  between operations  15.1 us (8%)
  blocking collectives  13 us (7%)
  matrix products  10.8 us (5%)
  other arithmetic  5.29 us (3%)
  local copies, waits for them, and re-layouts  4.84 us (2%)
    all_gather x1, waiting for transfers between devices, local(): lax.all_gather(jnp.concatenate([w_query, w_key, w_value], axis=1), 'dp',...  45.6 us
    all_to_all x1, waiting for transfers between devices, local(): lax.all_to_all(pick(wanted, table).astype(jnp.bfloat16).reshape(peers, ca...  33.6 us
    all_to_all x1, starting transfers between devices, local(): lax.all_to_all(requests, 'dp', split_axis=0, concat_axis=0, tiled=True)  20.4 us
    all_to_all x1, waiting for transfers between devices, local(): lax.all_to_all(requests, 'dp', split_axis=0, concat_axis=0, tiled=True)  14.1 us
    all_gather x1, blocking collectives, local(): lax.all_gather(norm_gain, 'mp', axis=0, tiled=True).astype(jnp.float32)  13 us
    ppermute x3, starting transfers between devices, local(): lax.ppermute(joined, 'mp', [(i, (i + k) % parts) for i in range(parts)])  10.6 us
    all_to_all x1, starting transfers between devices, local(): lax.all_to_all(grad_buffer.reshape(peers, capacity, col_width), 'dp', spl...  9.53 us
    all_to_all x1, waiting for transfers between devices, local(): lax.all_to_all(grad_buffer.reshape(peers, capacity, col_width), 'dp', spl...  7.74 us
  transfers between devices with their start and end apart: 7, of which 4 were waited for; matrix products, arithmetic and copies ran while one was open for 6% of the time, Pallas kernels for 0%

commit v1 on v0

--- a/solution.py
+++ b/solution.py
@@ -115,7 +115,9 @@
         ],
         axis=1,
     ).astype(jnp.float32)
-    gain = lax.all_gather(norm_gain, "mp", axis=0, tiled=True).astype(jnp.float32)
+    gain = jnp.concatenate(
+        lax.all_to_all(jnp.stack([norm_gain] * lax.axis_size("mp")), "mp", 0, 0), axis=0
+    ).astype(jnp.float32)
     scale = lax.rsqrt(jnp.mean(features * features, axis=1, keepdims=True) + 1e-06)
     normed = (features * scale * gain[None, :]).astype(jnp.bfloat16)
     projected = jnp.dot(normed, weights, preferred_element_type=jnp.float32).astype(jnp.bfloat16)

time: 197 us -> 203 us (1.030)
  waiting for transfers between devices: 101 us -> 115 us
  blocking collectives: 13 us -> 0 us
  starting transfers between devices: 46.2 us -> 49.9 us
    all_gather x1 -> x0, blocking collectives: 13 us -> none  [local(): lax.all_gather(norm_gain, 'mp', axis=0, tiled=True).astype(jnp.float32)]
    all_to_all x1, waiting for transfers between devices: 7.74 us -> 17.3 us  [local(): lax.all_to_all(grad_buffer.reshape(peers, capacity, col_width), 'dp', spl...]
    ppermute x3, waiting for transfers between devices: 0.01 us -> 9.33 us  [local(): lax.ppermute(joined, 'mp', [(i, (i + k) % parts) for i in range(parts)])]
    all_gather x1, waiting for transfers between devices: 45.6 us -> 39.5 us  [local(): lax.all_gather(jnp.concatenate([w_query, w_key, w_value], axis=1), 'dp',...]
    all_to_all x0 -> x1, starting transfers between devices: none -> 4.03 us  [local(): lax.all_to_all(jnp.stack([norm_gain] * lax.axis_size('mp')), 'mp', 0, 0)]
    all_to_all x0 -> x1, waiting for transfers between devices: none -> 2.67 us  [local(): lax.all_to_all(jnp.stack([norm_gain] * lax.axis_size('mp')), 'mp', 0, 0)]
  transfers between devices with their start and end apart: 7 -> 8, of which waited for: 4 -> 8; matrix products, arithmetic and copies ran while one was open for 6% -> 7% of each run, Pallas kernels for 0% -> 0%
where the time goes in v1:
time: 203 us
  waiting for transfers between devices  115 us (57%)
  starting transfers between devices  49.9 us (25%)
  between operations  15 us (7%)
  matrix products  10.8 us (5%)
  other arithmetic  5.99 us (3%)
  local copies, waits for them, and re-layouts  5.98 us (3%)
    all_gather x1, waiting for transfers between devices, local(): lax.all_gather(jnp.concatenate([w_query, w_key, w_value], axis=1), 'dp',...  39.5 us
    all_to_all x1, waiting for transfers between devices, local(): lax.all_to_all(pick(wanted, table).astype(jnp.bfloat16).reshape(peers, ca...  32.2 us
    all_to_all x1, starting transfers between devices, local(): lax.all_to_all(requests, 'dp', split_axis=0, concat_axis=0, tiled=True)  20.4 us
    all_to_all x1, waiting for transfers between devices, local(): lax.all_to_all(grad_buffer.reshape(peers, capacity, col_width), 'dp', spl...  17.3 us
    all_to_all x1, waiting for transfers between devices, local(): lax.all_to_all(requests, 'dp', split_axis=0, concat_axis=0, tiled=True)  14.1 us
    all_to_all x1, starting transfers between devices, local(): lax.all_to_all(grad_buffer.reshape(peers, capacity, col_width), 'dp', spl...  10.9 us
    ppermute x3, waiting for transfers between devices, local(): lax.ppermute(joined, 'mp', [(i, (i + k) % parts) for i in range(parts)])  9.33 us
    ppermute x3, starting transfers between devices, local(): lax.ppermute(joined, 'mp', [(i, (i + k) % parts) for i in range(parts)])  8.84 us
  transfers between devices with their start and end apart: 8, of which 8 were waited for; matrix products, arithmetic and copies ran while one was open for 7% of the time, Pallas kernels for 0%

profile of v1, /device:TPU:1, one launch (start us, length us, event | category | flops | bytes accessed | tf_op | source)
XLA Modules:
  0.0 202.9 jit_solution(6667498948460766797)
XLA Ops:
  7.2 1.5 pad_maximum_fusion.3
  8.7 0.9 convert_reduce_fusion
  11.2 20.4 %all-to-all-start = ((s32[128,1,2]{2,1,0:T(1,128)}), s32[128,1,2]{2,1,0:T(1,128)S(1)}, u32[]{:S(2)}, u32[]{:S(2)}) async-start(s32[128,1,2]{2,1,0:T(1,128)} %bitcast.4), calls=%async_computation | async-start | bytes 131072 | tf_op jit(solution)/shard_map/all_to_all | solution.py:75
  32.3 14.1 %all-to-all-done = s32[128,1,2]{2,1,0:T(1,128)S(1)} async-done(((s32[128,1,2]{2,1,0:T(1,128)}), s32[128,1,2]{2,1,0:T(1,128)S(1)}, u32[]{:S(2)}, u32[]{:S(2)}) %all-to-all-start) | async-done | bytes 1056 | tf_op jit(solution)/shard_map/all_to_all | solution.py:75
  47.0 0.8 reduce.3
  47.9 1.7 convolution_convert_fusion.1
  49.6 1.0 reshape.125
  50.6 5.7 %all-to-all-start.1 = ((bf16[128,2,1024]{2,1,0:T(2,128)(2,1)}), bf16[128,2,1024]{2,1,0:T(2,128)(2,1)S(1)}, u32[]{:S(2)}, u32[]{:S(2)}) async-start(bf16[128,2,1024]{2,1,0:T(2,128)(2,1)} %reshape.125), calls=%async_computation.1 | async-start | bytes 1048576 | tf_op jit(solution)/shard_map/all_to_all | solution.py:82
  58.1 32.2 %all-to-all-done.1 = bf16[128,2,1024]{2,1,0:T(2,128)(2,1)S(1)} async-done(((bf16[128,2,1024]{2,1,0:T(2,128)(2,1)}), bf16[128,2,1024]{2,1,0:T(2,128)(2,1)S(1)}, u32[]{:S(2)}, u32[]{:S(2)}) %all-to-all-start.1) | async-done | bytes 524320 | tf_op jit(solution)/shard_map/all_to_all | solution.py:82
  90.3 4.0 %all-to-all-start.2 = ((bf16[4,2,512]{2,1,0:T(2,128)(2,1)}), bf16[4,2,512]{2,1,0:T(2,128)(2,1)S(1)}, u32[]{:S(2)}, u32[]{:S(2)}) async-start(bf16[4,2,512]{2,1,0:T(2,128)(2,1)} %reshape.142), calls=%async_computation.2 | async-start | bytes 16384 | tf_op jit(solution)/shard_map/all_to_all | solution.py:119
  94.8 1.0 reshape.130
  95.8 2.7 %all-to-all-done.2 = bf16[4,2,512]{2,1,0:T(2,128)(2,1)S(1)} async-done(((bf16[4,2,512]{2,1,0:T(2,128)(2,1)}), bf16[4,2,512]{2,1,0:T(2,128)(2,1)S(1)}, u32[]{:S(2)}, u32[]{:S(2)}) %all-to-all-start.2) | async-done | bytes 8224 | tf_op jit(solution)/shard_map/all_to_all | solution.py:119
  98.5 10.9 %all-to-all-start.3 = ((bf16[128,2,1024]{2,1,0:T(2,128)(2,1)}), bf16[128,2,1024]{2,1,0:T(2,128)(2,1)S(1)}, u32[]{:S(2)}, u32[]{:S(2)}) async-start(bf16[128,2,1024]{2,1,0:T(2,128)(2,1)} %reshape.130), calls=%async_computation.3 | async-start | bytes 1048576 | tf_op jit(solution)/shard_map/all_to_all | solution.py:91
  110.3 2.2 %collective-permute-start = (bf16[128,1024]{1,0:T(8,128)(2,1)S(1)}, bf16[128,1024]{1,0:T(8,128)(2,1)S(1)}, u32[]{:S(2)}, u32[]{:S(2)}) collective-permute-start(bf16[128,1024]{1,0:T(8,128)(2,1)S(1)} %convolution_convert_fusion.3), channel_id=1, source_target_pairs={{0,1},{1,2},{2,3},{3,0},{4,5},{5,6},{6,7},{7,4},{8,9},{9,10},{10,1... | collective-permute-start | bytes 786440 | tf_op jit(solution)/shard_map/ppermute | solution.py:106
  112.5 3.7 %collective-permute-start.1 = (bf16[128,1024]{1,0:T(8,128)(2,1)S(1)}, bf16[128,1024]{1,0:T(8,128)(2,1)S(1)}, u32[]{:S(2)}, u32[]{:S(2)}) collective-permute-start(bf16[128,1024]{1,0:T(8,128)(2,1)S(1)} %convolution_convert_fusion.3), channel_id=1, source_target_pairs={{0,2},{1,3},{2,0},{3,1},{4,6},{5,7},{6,4},{7,5},{8,10},{9,11},{10,... | collective-permute-start | bytes 786440 | tf_op jit(solution)/shard_map/ppermute | solution.py:106
  116.2 3.0 %collective-permute-start.2 = (bf16[128,1024]{1,0:T(8,128)(2,1)S(1)}, bf16[128,1024]{1,0:T(8,128)(2,1)S(1)}, u32[]{:S(2)}, u32[]{:S(2)}) collective-permute-start(bf16[128,1024]{1,0:T(8,128)(2,1)S(1)} %convolution_convert_fusion.3), channel_id=1, source_target_pairs={{0,3},{1,0},{2,1},{3,2},{4,7},{5,4},{6,5},{7,6},{8,11},{9,8},{10,9... | collective-permute-start | bytes 786440 | tf_op jit(solution)/shard_map/ppermute | solution.py:106
  119.4 1.6 collective-permute-done
  121.0 4.3 %collective-permute-done.1 = bf16[128,1024]{1,0:T(8,128)(2,1)S(1)} collective-permute-done((bf16[128,1024]{1,0:T(8,128)(2,1)S(1)}, bf16[128,1024]{1,0:T(8,128)(2,1)S(1)}, u32[]{:S(2)}, u32[]{:S(2)}) %collective-permute-start.1) | collective-permute-done | bytes 262176 | tf_op jit(solution)/shard_map/ppermute | solution.py:106
  125.4 3.4 %collective-permute-done.2 = bf16[128,1024]{1,0:T(8,128)(2,1)S(1)} collective-permute-done((bf16[128,1024]{1,0:T(8,128)(2,1)S(1)}, bf16[128,1024]{1,0:T(8,128)(2,1)S(1)}, u32[]{:S(2)}, u32[]{:S(2)}) %collective-permute-start.2) | collective-permute-done | bytes 262176 | tf_op jit(solution)/shard_map/ppermute | solution.py:106
  129.3 17.3 %all-to-all-done.3 = bf16[128,2,1024]{2,1,0:T(2,128)(2,1)S(1)} async-done(((bf16[128,2,1024]{2,1,0:T(2,128)(2,1)}), bf16[128,2,1024]{2,1,0:T(2,128)(2,1)S(1)}, u32[]{:S(2)}, u32[]{:S(2)}) %all-to-all-start.3) | async-done | bytes 524320 | tf_op jit(solution)/shard_map/all_to_all | solution.py:91
  146.8 1.7 convert_multiply_fusion.4
  148.6 39.5 %all-gather.2.cloned.1.call-done = bf16[4096,1536]{1,0:T(8,128)(2,1)} async-done(((bf16[32,1536]{1,0:T(8,128)(2,1)}), bf16[4096,1536]{1,0:T(8,128)(2,1)}) %all-gather.2.cloned.1.call-update) | async-done | bytes 12582928 | tf_op jit(solution)/shard_map/all_gather | solution.py:64
  188.1 6.4 %convolution_convert_fusion = bf16[128,1536]{1,0:T(8,128)(2,1)S(1)} fusion(bf16[4096,1536]{1,0:T(8,128)(2,1)} %all-gather.2.cloned.1.call-done, f32[4096]{0:T(1024)S(1)} %bitcast.51, f32[128]{0:T(128)S(1)} %add_rsqrt_fusion, bf16[128,1024]{1,0:T(8,128)(2,1)S(1)} %get-tuple-element.22, bf16[128,1024]{1,0:T(8,128)(2,1)S(1)} %get-tuple-element.23, ...), kind=kOutput, calls=%fused_computation.3 | convolution fusion | flops 1616576512 | bytes 14041600 | tf_op jit(solution)/shard_map/dot_general | solution.py:123
  195.2 0.8 copy.36
  (41 shorter events, 7.1 us)
Async XLA Ops:
  7.2 87.2 %copy-start = (bf16[128,1024]{1,0:T(8,128)(2,1)S(1)}, bf16[128,1024]{1,0:T(8,128)(2,1)}, u32[]{:S(2)}) copy-start(bf16[128,1024]{1,0:T(8,128)(2,1)} %param.23) | copy-start | bytes 786436
  7.2 180.9 %all-gather.2.cloned.1.call-start = ((), (), s32[]{:S(2)}) async-start(), calls=%async_computation.4 | async-start | bytes 12681216 | tf_op jit(solution)/shard_map/all_gather | solution.py:64
  10.4 45.8 %copy-start.3 = (bf16[1024]{0:T(1024)(128)(2,1)S(1)}, bf16[1024]{0:T(1024)(128)(2,1)}, u32[]{:S(2)}) copy-start(bf16[1024]{0:T(1024)(128)(2,1)} %param.19) | copy-start | bytes 6148
  11.2 35.2 %all-to-all-start = ((s32[128,1,2]{2,1,0:T(1,128)}), s32[128,1,2]{2,1,0:T(1,128)S(1)}, u32[]{:S(2)}, u32[]{:S(2)}) async-start(s32[128,1,2]{2,1,0:T(1,128)} %bitcast.4), calls=%async_computation | async-start | bytes 131072 | tf_op jit(solution)/shard_map/all_to_all | solution.py:75
  50.6 39.7 %all-to-all-start.1 = ((bf16[128,2,1024]{2,1,0:T(2,128)(2,1)}), bf16[128,2,1024]{2,1,0:T(2,128)(2,1)S(1)}, u32[]{:S(2)}, u32[]{:S(2)}) async-start(bf16[128,2,1024]{2,1,0:T(2,128)(2,1)} %reshape.125), calls=%async_computation.1 | async-start | bytes 1048576 | tf_op jit(solution)/shard_map/all_to_all | solution.py:82
  56.3 53.8 %copy-start.4 = (s32[128,1]{0,1:T(1,128)S(1)}, s32[128,1]{0,1:T(1,128)}, u32[]{:S(2)}) copy-start(s32[128,1]{0,1:T(1,128)} %param.13) | copy-start | bytes 1540
  90.3 8.2 %all-to-all-start.2 = ((bf16[4,2,512]{2,1,0:T(2,128)(2,1)}), bf16[4,2,512]{2,1,0:T(2,128)(2,1)S(1)}, u32[]{:S(2)}, u32[]{:S(2)}) async-start(bf16[4,2,512]{2,1,0:T(2,128)(2,1)} %reshape.142), calls=%async_computation.2 | async-start | bytes 16384 | tf_op jit(solution)/shard_map/all_to_all | solution.py:119
  98.5 48.1 %all-to-all-start.3 = ((bf16[128,2,1024]{2,1,0:T(2,128)(2,1)}), bf16[128,2,1024]{2,1,0:T(2,128)(2,1)S(1)}, u32[]{:S(2)}, u32[]{:S(2)}) async-start(bf16[128,2,1024]{2,1,0:T(2,128)(2,1)} %reshape.130), calls=%async_computation.3 | async-start | bytes 1048576 | tf_op jit(solution)/shard_map/all_to_all | solution.py:91
  110.3 10.7 %collective-permute-start = (bf16[128,1024]{1,0:T(8,128)(2,1)S(1)}, bf16[128,1024]{1,0:T(8,128)(2,1)S(1)}, u32[]{:S(2)}, u32[]{:S(2)}) collective-permute-start(bf16[128,1024]{1,0:T(8,128)(2,1)S(1)} %convolution_convert_fusion.3), channel_id=1, source_target_pairs={{0,1},{1,2},{2,3},{3,0},{4,5},{5,6},{6,7},{7,4},{8,9},{9,10},{10,1... | collective-permute-start | bytes 786440 | tf_op jit(solution)/shard_map/ppermute | solution.py:106
  112.5 12.9 %collective-permute-start.1 = (bf16[128,1024]{1,0:T(8,128)(2,1)S(1)}, bf16[128,1024]{1,0:T(8,128)(2,1)S(1)}, u32[]{:S(2)}, u32[]{:S(2)}) collective-permute-start(bf16[128,1024]{1,0:T(8,128)(2,1)S(1)} %convolution_convert_fusion.3), channel_id=1, source_target_pairs={{0,2},{1,3},{2,0},{3,1},{4,6},{5,7},{6,4},{7,5},{8,10},{9,11},{10,... | collective-permute-start | bytes 786440 | tf_op jit(solution)/shard_map/ppermute | solution.py:106
  116.2 12.5 %collective-permute-start.2 = (bf16[128,1024]{1,0:T(8,128)(2,1)S(1)}, bf16[128,1024]{1,0:T(8,128)(2,1)S(1)}, u32[]{:S(2)}, u32[]{:S(2)}) collective-permute-start(bf16[128,1024]{1,0:T(8,128)(2,1)S(1)} %convolution_convert_fusion.3), channel_id=1, source_target_pairs={{0,3},{1,0},{2,1},{3,2},{4,7},{5,4},{6,5},{7,6},{8,11},{9,8},{10,9... | collective-permute-start | bytes 786440 | tf_op jit(solution)/shard_map/ppermute | solution.py:106
  128.9 17.9 %copy-start.1 = (bf16[256,1024]{1,0:T(8,128)(2,1)S(1)}, bf16[256,1024]{1,0:T(8,128)(2,1)}, u32[]{:S(2)}) copy-start(bf16[256,1024]{1,0:T(8,128)(2,1)} %param.16) | copy-start | bytes 1572868
  128.9 17.9 %copy-start.2 = (bf16[256,1024]{1,0:T(8,128)(2,1)S(1)}, bf16[256,1024]{1,0:T(8,128)(2,1)}, u32[]{:S(2)}) copy-start(bf16[256,1024]{1,0:T(8,128)(2,1)} %param.15) | copy-start | bytes 1572868
Sparse Core Ops, SparseCore 0:
  11.7 176.3 all-gather.1
